TPU v7x, 512 devices: a whole 4x8x8 slice. The times are simulated.
512 devices in a mesh: rep: 64 (over x, z_hi, y), ctx: 8 (over z_lo, core).
Axes of the slice: x: 4, y: 8, z: 8 (z_hi: 2, z_lo: 4; z = z_hi * 4 + z_lo), core: 2. Of those that a mesh axis runs over, the one named last changes fastest.
Arguments:
- activations: bfloat16 [64, 1024, 4096], P('rep', 'ctx'), may hold values from -6 to 6
- queries: bfloat16 [64, 1024, 2048], P('rep', 'ctx'), may hold values from -110 to 110
- key_states: bfloat16 [64, 1024, 512], P('rep', 'ctx'), may hold values from -4 to 4
- targets: bfloat16 [64, 1024, 2048], P('rep', 'ctx'), may hold values from -1.5 to 1.5
- value_weight: bfloat16 [64, 4096, 512], P('rep', 'ctx'), may hold values from -5 to 5
- tracker: bfloat16 [64, 4096, 512], P('rep', 'ctx'), may hold values from -5 to 5
- old_gradient: bfloat16 [64, 4096, 512], P('rep', 'ctx'), may hold values from -5 to 5
Outputs:
- new_weight: bfloat16 [64, 4096, 512], P('rep', 'ctx')
- new_tracker: bfloat16 [64, 4096, 512], P('rep', 'ctx')
All inputs are finite; a program needn't handle non-finite values.
Results may differ from a plain program's by a relative error of at most 0.0095.
Values may be sent and summed in bfloat16 or wider, within the bound.
A program may use at most 64 MiB of HBM per device.

v0:
```python
import jax
import jax.numpy as jnp
from jax import lax
from jax.sharding import PartitionSpec as P

HEADS = 16
KV_HEADS = 4
HEAD_DIM = 128
ROUND = 3


step_size = 0.25
loss_weight = 16.0


def partner(shard, axis, apart):
    return lax.ppermute(shard, axis, [(i, i ^ 1 << apart) for i in range(lax.axis_size(axis))])


def local(activations, queries, key_states, targets, value_weight, tracker, old_gradient):
    token_block = activations[0]
    tokens_here = token_block.shape[0]
    value_scale = token_block.shape[1] ** (-0.5)
    grouping = HEADS // KV_HEADS
    own_weight = value_weight[0]
    weight_full = own_weight.astype(jnp.float32)
    track_full = tracker[0].astype(jnp.float32)
    old_full = old_gradient[0].astype(jnp.float32)
    feature_cols = lax.all_to_all(token_block, "ctx", split_axis=1, concat_axis=0, tiled=True)
    local_values = (
        jnp.dot(
            token_block,
            lax.all_gather(own_weight, "ctx", axis=0, tiled=True),
            preferred_element_type=jnp.float32,
        )
        * value_scale
    ).astype(jnp.bfloat16)
    all_keys, all_values = (
        lax.all_gather(key_states[0], "ctx", axis=0, tiled=True),
        lax.all_gather(local_values, "ctx", axis=0, tiled=True),
    )
    seq_total = all_keys.shape[0]
    query_heads = queries[0].reshape(tokens_here, KV_HEADS, grouping, HEAD_DIM)
    key_heads = all_keys.reshape(seq_total, KV_HEADS, HEAD_DIM)
    value_heads = all_values.reshape(seq_total, KV_HEADS, HEAD_DIM)
    scores = jnp.einsum(
        "ikgd,jkd->kgij", query_heads, key_heads, preferred_element_type=jnp.float32
    ) * HEAD_DIM ** (-0.5)
    query_pos = lax.axis_index("ctx") * tokens_here + jnp.arange(tokens_here)
    key_pos = jnp.arange(seq_total)
    allowed = key_pos[None, :] <= query_pos[:, None]
    scores = jnp.where(allowed, scores, -jnp.inf)
    highest = jnp.max(scores, axis=-1, keepdims=True)
    raised = jnp.exp(scores - highest)
    probabilities = (raised / jnp.sum(raised, axis=-1, keepdims=True)).astype(jnp.bfloat16)
    attended = jnp.einsum(
        "kgij,jkd->ikgd", probabilities, value_heads, preferred_element_type=jnp.float32
    )
    attended = attended.reshape(tokens_here, HEADS * HEAD_DIM)
    out_cot = (loss_weight * (attended - targets[0].astype(jnp.float32))).astype(jnp.bfloat16)
    cot_heads = out_cot.reshape(tokens_here, KV_HEADS, grouping, HEAD_DIM)
    value_terms = jnp.einsum(
        "kgij,ikgd->jkd", probabilities, cot_heads, preferred_element_type=jnp.float32
    )
    value_terms = value_terms.reshape(seq_total, KV_HEADS * HEAD_DIM)
    value_cot16 = lax.psum(value_terms, "ctx").astype(jnp.bfloat16)
    gradient = (
        jnp.einsum("tc,tv->cv", feature_cols, value_cot16, preferred_element_type=jnp.float32)
        * value_scale
    )
    track_half = track_full + gradient - old_full
    moved = weight_full - step_size * track_half
    peer_both = partner(jnp.stack((moved, track_half)), "rep", ROUND)
    new_weight = ((moved + peer_both[0]) * 0.5).astype(jnp.bfloat16)
    new_tracker = ((track_half + peer_both[1]) * 0.5).astype(jnp.bfloat16)
    return (new_weight[None], new_tracker[None])


def solution(mesh):
    return jax.shard_map(
        local,
        mesh=mesh,
        in_specs=(
            P("rep", "ctx", None),
            P("rep", "ctx", None),
            P("rep", "ctx", None),
            P("rep", "ctx", None),
            P("rep", "ctx", None),
            P("rep", "ctx", None),
            P("rep", "ctx", None),
        ),
        out_specs=(P("rep", "ctx", None), P("rep", "ctx", None)),
        check_vma=False,
    )
```

profile of v0, /device:TPU:1, one launch (start us, length us, event | category | flops | bytes accessed | tf_op | source)
XLA Modules:
  0.0 347.0 jit_solution(10551125804644642913)
XLA Ops:
  7.2 0.7 all-gather.8.cloned.1.call-update
  8.0 1.7 copy.29
  9.7 2.3 copy.36
  11.9 10.3 %all-to-all-start = ((bf16[128,8,512]{0,2,1:T(8,128)(2,1)}), bf16[128,8,512]{0,2,1:T(8,128)(2,1)S(1)}, u32[]{:S(2)}, u32[]{:S(2)}) async-start(bf16[128,8,512]{0,2,1:T(8,128)(2,1)} %bitcast.16), calls=%async_computation | async-start | bytes 2097152 | tf_op jit(solution)/shard_map/all_to_all | solution.py:29
  22.2 64.3 %all-gather.8.cloned.1.call-done = bf16[1,4096,512]{2,1,0:T(8,128)(2,1)} async-done(((bf16[1,512,512]{2,1,0:T(8,128)(2,1)}), bf16[1,4096,512]{2,1,0:T(8,128)(2,1)}) %all-gather.8.cloned.1.call-update) | async-done | bytes 4194320 | tf_op jit(solution)/shard_map/all_gather | solution.py:33
  86.6 3.9 %fusion.19 = bf16[128,512]{1,0:T(8,128)(2,1)} fusion(bf16[1,4096,512]{2,1,0:T(8,128)(2,1)} %all-gather.8.cloned.1.call-done, bf16[1,128,4096]{2,1,0:T(8,128)(2,1)} %param.7), kind=kOutput, calls=%fused_computation.22 | convolution fusion | flops 537001984 | bytes 5373952 | tf_op jit(solution)/shard_map/dot_general | solution.py:31
  90.7 1.2 reshape_squeeze.3
  91.9 1.2 copy.34
  93.1 1.3 copy.28
  94.3 2.0 copy.38
  96.5 1.4 copy.37
  97.8 27.6 %all-gather.10.cloned.1.call-done = bf16[1,1024,512]{1,2,0:T(8,128)(2,1)} async-done(((bf16[1,128,512]{1,2,0:T(8,128)(2,1)}), bf16[1,1024,512]{1,2,0:T(8,128)(2,1)}) %all-gather.10.cloned.1.call-update) | async-done | bytes 1048592 | tf_op jit(solution)/shard_map/all_gather | solution.py:39
  125.4 7.3 %fusion.44 = (f32[4,4,128]{2,1,0:T(4,128)S(1)}, f32[4,4,128,1024]{2,3,1,0:T(8,128)}) fusion(pred[128,1024]{0,1:T(8,128)(4,1)S(1)} %iota_compare_fusion, bf16[1024,4,128,1]{0,2,3,1:T(8,128)(2,1)} %bitcast.105, bf16[128,4,4,128]{3,2,1,0:T(4,128)(2,1)} %reshape_squeeze.3), kind=kOutput, calls=%fused_computation.46 | convolution fusion | flops 545260544 | bytes 10100736 | tf_op jit(solution)/shard_map/sub | solution.py:54
  132.7 31.0 %all-gather.6.cloned.1.call-done = bf16[1024,512]{1,0:T(8,128)(2,1)} async-done(((bf16[128,512]{1,0:T(8,128)(2,1)}), bf16[1024,512]{1,0:T(8,128)(2,1)}) %all-gather.6.cloned.1.call-update) | async-done | bytes 1048592 | tf_op jit(solution)/shard_map/all_gather | solution.py:40
  163.6 2.3 copy.46
  165.9 8.5 %fusion.15 = f32[4,128,1024,1]{2,1,3,0:T(8,128)S(1)} fusion(f32[128,4,4,128]{0,3,2,1:T(8,128)} %bitcast.102, bf16[1024,4,128,1]{0,2,3,1:T(8,128)(2,1)} %bitcast.104, f32[4,4,128,1024]{2,3,1,0:T(8,128)} %get-tuple-element.11, f32[4,4,128]{2,1,0:T(4,128)S(1)} %get-tuple-element.10), kind=kOutput, calls=%fused_computation.20 | convolution fusion | flops 1082916864 | bytes 12591104 | tf_op jit(solution)/shard_map/kgij,ikgd->jkd/dot_general | solution.py:62
  174.4 62.7 %all-reduce.1 = bf16[1024,512]{0,1:T(8,128)(2,1)} all-reduce(f32[1024,512]{0,1:T(8,128)S(1)} %bitcast.101), channel_id=1, replica_groups=mesh['rep'=64,'ctx'=8] {'ctx'}, use_global_device_ids=true, to_apply=%region_2.3 | all-reduce | flops 524288 | bytes 3145728 | tf_op jit(solution)/shard_map/psum | solution.py:66
  237.1 2.4 fusion.13
  239.7 0.2 pad_maximum_fusion
  239.9 6.0 %collective-permute-start = (f32[2,512,512]{1,2,0:T(8,128)S(1)}, f32[2,512,512]{1,2,0:T(8,128)S(1)}, u32[]{:S(2)}, u32[]{:S(2)}) collective-permute-start(f32[2,512,512]{1,2,0:T(8,128)S(1)} %pad_maximum_fusion), channel_id=1, source_target_pairs={{0,64},{8,72},{16,80},{24,88},{32,96},{40,104},{48,112},{56,120},{... | collective-permute-start | bytes 6291464 | tf_op jit(solution)/shard_map/ppermute | solution.py:17
  245.9 92.1 %collective-permute-done = f32[2,512,512]{1,2,0:T(8,128)S(1)} collective-permute-done((f32[2,512,512]{1,2,0:T(8,128)S(1)}, f32[2,512,512]{1,2,0:T(8,128)S(1)}, u32[]{:S(2)}, u32[]{:S(2)}) %collective-permute-start) | collective-permute-done | bytes 2097184 | tf_op jit(solution)/shard_map/ppermute | solution.py:17
  338.0 0.5 fusion.32
  338.5 1.0 copy.39
  339.5 1.0 copy.40
  (16 shorter events, 0.6 us)
Async XLA Ops:
  7.2 83.3 %copy-start = (bf16[1,512,512]{2,1,0:T(8,128)(2,1)S(1)}, bf16[1,512,512]{2,1,0:T(8,128)(2,1)}, u32[]{:S(2)}) copy-start(bf16[1,512,512]{2,1,0:T(8,128)(2,1)} %param.11) | copy-start | bytes 1572868
  7.2 83.5 %copy-start.2 = (bf16[1,128,2048]{2,1,0:T(8,128)(2,1)S(1)}, bf16[1,128,2048]{2,1,0:T(8,128)(2,1)}, u32[]{:S(2)}) copy-start(bf16[1,128,2048]{2,1,0:T(8,128)(2,1)} %param.8) | copy-start | bytes 1572868
  7.2 84.7 %copy-start.1 = (bf16[1,128,2048]{2,1,0:T(8,128)(2,1)S(1)}, bf16[1,128,2048]{2,1,0:T(8,128)(2,1)}, u32[]{:S(2)}) copy-start(bf16[1,128,2048]{2,1,0:T(8,128)(2,1)} %param.10) | copy-start | bytes 1572868
  7.2 79.4 %all-gather.8.cloned.1.call-start = ((), (), s32[]{:S(2)}) async-start(), calls=%async_computation.2 | async-start | bytes 4718592 | tf_op jit(solution)/shard_map/all_gather | solution.py:33
  7.9 117.5 %all-gather.10.cloned.1.call-start = ((), (), s32[]{:S(2)}) async-start(), calls=%async_computation.3 | async-start | bytes 1179648 | tf_op jit(solution)/shard_map/all_gather | solution.py:39
  11.9 84.5 %all-to-all-start = ((bf16[128,8,512]{0,2,1:T(8,128)(2,1)}), bf16[128,8,512]{0,2,1:T(8,128)(2,1)S(1)}, u32[]{:S(2)}, u32[]{:S(2)}) async-start(bf16[128,8,512]{0,2,1:T(8,128)(2,1)} %bitcast.16), calls=%async_computation | async-start | bytes 2097152 | tf_op jit(solution)/shard_map/all_to_all | solution.py:29
  22.2 141.4 %all-gather.6.cloned.1.call-start = ((), (), s32[]{:S(2)}) async-start(), calls=%async_computation.1 | async-start | bytes 1179648 | tf_op jit(solution)/shard_map/all_gather | solution.py:40
  239.9 98.1 %collective-permute-start = (f32[2,512,512]{1,2,0:T(8,128)S(1)}, f32[2,512,512]{1,2,0:T(8,128)S(1)}, u32[]{:S(2)}, u32[]{:S(2)}) collective-permute-start(f32[2,512,512]{1,2,0:T(8,128)S(1)} %pad_maximum_fusion), channel_id=1, source_target_pairs={{0,64},{8,72},{16,80},{24,88},{32,96},{40,104},{48,112},{56,120},{... | collective-permute-start | bytes 6291464 | tf_op jit(solution)/shard_map/ppermute | solution.py:17
Sparse Core Ops, SparseCore 0:
  10.1 76.4 all-gather.7
  88.6 36.7 all-gather.9
  127.5 36.1 all-gather.5
where the time goes:
time: 347 us
  waiting for transfers between devices  216 us (62%)
  blocking collectives  62.7 us (18%)
  matrix products  22 us (6%)
  starting transfers between devices  16.4 us (5%)
  local copies, waits for them, and re-layouts  15.5 us (4%)
  between operations  13.8 us (4%)
    ppermute x1, waiting for transfers between devices, partner(): lax.ppermute(shard, axis, [(i, i ^ 1 << apart) for i in range(lax.axis_si...  92.1 us
    all_gather x1, waiting for transfers between devices, local(): lax.all_gather(own_weight, 'ctx', axis=0, tiled=True)  64.3 us
    psum x1, blocking collectives, local(): value_cot16 = lax.psum(value_terms, 'ctx').astype(jnp.bfloat16)  62.7 us
    all_gather x1, waiting for transfers between devices, local(): lax.all_gather(local_values, 'ctx', axis=0, tiled=True)  31 us
    all_gather x1, waiting for transfers between devices, local(): lax.all_gather(key_states[0], 'ctx', axis=0, tiled=True)  27.6 us
    all_to_all x1, starting transfers between devices, local(): lax.all_to_all(token_block, 'ctx', split_axis=1, concat_axis=0, tiled=True)  10.3 us
    unnamed x13, local copies, waits for them, and re-layouts  9.48 us
    dot_general x1, matrix products, local(): jnp.einsum('kgij,ikgd->jkd', probabilities, cot_heads, preferred_element_...  8.46 us
  transfers between devices with their start and end apart: 5, of which 4 were waited for; matrix products, arithmetic and copies ran while one was open for 6% of the time, Pallas kernels for 0%

commit v1 on v0

v1 whole, which is shorter than its diff:
```python
import functools

import jax
import jax.numpy as jnp
from jax import lax
from jax.experimental import pallas as pl
from jax.experimental.pallas import tpu as pltpu
from jax.sharding import PartitionSpec as P

ROUND = 3
STEP = 0.25
LOSS = 16.0
CTX = 8
CHIPS = 4
ROWS = 128
SEQ = 1024
HALF = 512
D = 4096
FEAT = 512
COLS = 512
HD = 128
QB = 256
LOG2E = 1.4426950408889634
F32 = jnp.float32
BF16 = jnp.bfloat16
MESH = pl.DeviceIdType.MESH


def dot(a, b):
    return jnp.dot(a, b, preferred_element_type=F32)


def dot_nt(a, b):
    return lax.dot_general(a, b, (((1,), (1,)), ((), ())), preferred_element_type=F32)


def kernel(
    a_h, q_h, k_h, t_h, w_h, tr_h, og_h,
    nw_ref, nt_ref,
    abuf, qbuf, kbuf, tbuf, wv, trv, ogv, ft, psend, pown, precv, sums, rbuf,
    v, vt, acc, trecv, vc, th, th16, thp, wp,
    a_s, a_r, q_s, q_r, k_s, k_r, t_s, t_r, w_s, w_r, p_s, p_r, r_s, r_r,
    v_s, v_r, c_s, c_r, b_s, b_r, f_s, f_r, x_s, x_r, loc,
):
    me = lax.axis_index("ctx")
    rep = lax.axis_index("rep")
    i = lax.div(me, 2)
    s = lax.rem(me, 2)
    mate = me + 1 - 2 * s
    apart = 1 << ROUND
    peer = rep + apart * (1 - 2 * lax.rem(lax.div(rep, apart), 2))

    def lanes(n, size):
        return pl.ds(pl.multiple_of(n * size, size), size)

    def remote(src, dst, ss, rs, ctx, r=None):
        return pltpu.make_async_remote_copy(
            src_ref=src, dst_ref=dst, send_sem=ss, recv_sem=rs,
            device_id=(rep if r is None else r, ctx), device_id_type=MESH,
        )

    def arrived(ref, sem):
        pltpu.make_async_copy(ref, ref, sem).wait()

    barrier = pltpu.get_barrier_semaphore()
    for k in range(1, CTX):
        pl.semaphore_signal(barrier, inc=1, device_id=(rep, lax.rem(me + k, CTX)), device_id_type=MESH)
    pl.semaphore_signal(barrier, inc=1, device_id=(peer, me), device_id_type=MESH)

    mine = lanes(me, ROWS)
    own = [
        pltpu.make_async_copy(w_h, wv, loc.at[0]),
        pltpu.make_async_copy(a_h.at[:, lanes(me, FEAT)], abuf.at[me], a_r.at[me]),
        pltpu.make_async_copy(q_h.at[:, lanes(me, 2 * HD)], qbuf.at[mine], q_r.at[me]),
        pltpu.make_async_copy(k_h.at[:, lanes(i, HD)], kbuf.at[mine], k_r.at[me]),
        pltpu.make_async_copy(t_h.at[:, lanes(me, 2 * HD)], tbuf.at[mine], t_r.at[me]),
        pltpu.make_async_copy(tr_h, trv, loc.at[1]),
        pltpu.make_async_copy(og_h, ogv, loc.at[2]),
    ]
    for copy in own:
        copy.start()

    pl.semaphore_wait(barrier, CTX)

    sends = []

    def send(*args):
        copy = remote(*args)
        copy.start()
        sends.append(copy)

    order = (4, 3, 5, 2, 6, 1, 7)
    for k in order:
        p = lax.rem(me + k, CTX)
        send(a_h.at[:, lanes(p, FEAT)], abuf.at[me], a_s.at[k], a_r.at[me], p)
    for k in order:
        p = lax.rem(me + k, CTX)
        send(k_h.at[:, lanes(lax.div(p, 2), HD)], kbuf.at[mine], k_s.at[k], k_r.at[me], p)
    for k in order:
        p = lax.rem(me + k, CTX)
        send(q_h.at[:, lanes(p, 2 * HD)], qbuf.at[mine], q_s.at[k], q_r.at[me], p)
    for k in order:
        p = lax.rem(me + k, CTX)
        send(t_h.at[:, lanes(p, 2 * HD)], tbuf.at[mine], t_s.at[k], t_r.at[me], p)

    own[0].wait()
    for m in range(4):
        j = 4 * (1 - s) + m
        arrived(abuf.at[j], a_r.at[j])
        psend[m] = dot(abuf[j], wv[...])
        send(psend.at[m], precv.at[m], p_s.at[m], p_r.at[m], mate)
        ft[:, lanes(j, ROWS)] = abuf[j].T
    for m in range(4):
        j = 4 * s + m
        arrived(abuf.at[j], a_r.at[j])
        pown[m] = dot(abuf[j], wv[...])
        ft[:, lanes(j, ROWS)] = abuf[j].T
    for m in range(4):
        arrived(precv.at[m], p_r.at[m])
        total = pown[m] + precv[m]
        for k in range(CHIPS):
            sums[k, m * ROWS:(m + 1) * ROWS, :] = total[:, k * HD:(k + 1) * HD].astype(BF16)
    for k in (2, 1, 3):
        kc = lax.rem(i + k, CHIPS)
        send(sums.at[kc], rbuf.at[i], r_s.at[k], r_r.at[i], 2 * kc + s)
    send(w_h, wp, w_s.at[0], w_r.at[0], me, peer)
    for k in range(1, CHIPS):
        src = lax.rem(i + k, CHIPS)
        arrived(rbuf.at[src], r_r.at[src])
    for m in range(4):
        rows = slice(m * ROWS, (m + 1) * ROWS)
        total = pown[m, :, lanes(i, HD)] + precv[m, :, lanes(i, HD)]
        for k in range(1, CHIPS):
            total = total + rbuf[lax.rem(i + k, CHIPS), rows, :].astype(F32)
        v[s, rows, :] = (total * D ** -0.5).astype(BF16)
    send(v.at[s], v.at[s], v_s.at[0], v_r.at[0], mate)
    arrived(v.at[1 - s], v_r.at[0])
    for h in range(2):
        vt[:, h * HALF:(h + 1) * HALF] = v[h].T

    for j in range(CTX):
        rows = slice(j * ROWS, (j + 1) * ROWS)
        arrived(kbuf.at[rows], k_r.at[j])
        arrived(qbuf.at[rows], q_r.at[j])
        arrived(tbuf.at[rows], t_r.at[j])
    acc[...] = jnp.zeros_like(acc)
    later = lax.broadcasted_iota(jnp.int32, (QB, QB), 0) > lax.broadcasted_iota(jnp.int32, (QB, QB), 1)

    def head(g, carry):
        cols = lanes(g, HD)
        for b in range(SEQ // QB):
            at = slice(b * QB, (b + 1) * QB)
            upto = (b + 1) * QB
            scores = dot_nt(kbuf[:upto, :], qbuf[at, cols])
            edge = jnp.where(later, -jnp.inf, scores[b * QB:, :])
            scores = jnp.concatenate((scores[:b * QB, :], edge), axis=0) if b else edge
            highest = jnp.max(scores, axis=0, keepdims=True)
            raised = jnp.exp2((scores - highest) * (HD ** -0.5 * LOG2E))
            share = 1.0 / jnp.sum(raised, axis=0, keepdims=True)
            prob = (raised * share).astype(BF16)
            attended = dot(vt[:, :upto], prob).T
            cot = (LOSS * (attended - tbuf[at, cols].astype(F32))).astype(BF16)
            acc[:upto, :] += dot(prob, cot)
        return carry

    lax.fori_loop(0, 2, head, 0)

    half = pl.ds(pl.multiple_of(s * HALF, HALF), HALF)
    other = pl.ds(pl.multiple_of((1 - s) * HALF, HALF), HALF)
    send(acc.at[other], trecv, c_s.at[0], c_r.at[0], mate)
    arrived(trecv, c_r.at[0])
    vc[i, half, :] = (acc[half, :] + trecv[...]).astype(BF16)
    block = vc.at[i, half]
    send(block, block, f_s.at[0], f_r.at[i], mate)
    for k in (2, 1, 3):
        send(block, block, b_s.at[k], b_r.at[i], 2 * lax.rem(i + k, CHIPS) + s)

    own[5].wait()
    own[6].wait()
    for k in range(CHIPS):
        h = lax.rem(i + k, CHIPS)
        if k:
            landed = vc.at[h, half]
            arrived(landed, b_r.at[h])
            send(landed, landed, f_s.at[k], f_r.at[h], mate)
        arrived(vc.at[h, other], f_r.at[h])
        cols = lanes(h, HD)
        gradient = dot(ft[...], vc[h]) * D ** -0.5
        stepped = trv[:, cols].astype(F32) + gradient - ogv[:, cols].astype(F32)
        th[h] = stepped
        th16[h] = stepped.astype(BF16)
        send(th16.at[h], thp.at[h], x_s.at[k], x_r.at[h], me, peer)

    arrived(wp, w_r.at[0])
    for k in range(CHIPS):
        h = lax.rem(i + k, CHIPS)
        cols = lanes(h, HD)
        arrived(thp.at[h], x_r.at[h])
        mixed = (th[h] + thp[h].astype(F32)) * 0.5
        nt_ref[:, cols] = mixed.astype(BF16)
        nw_ref[:, cols] = (
            (wv[:, cols].astype(F32) + wp[:, cols].astype(F32)) * 0.5 - STEP * mixed
        ).astype(BF16)
    for copy in sends:
        copy.wait_send()


def local(activations, queries, key_states, targets, value_weight, tracker, old_gradient):
    dma = lambda n: pltpu.SemaphoreType.DMA((n,))
    shape = jax.ShapeDtypeStruct((FEAT, COLS), BF16)
    new_weight, new_tracker = pl.pallas_call(
        kernel,
        out_shape=(shape, shape),
        in_specs=[pl.BlockSpec(memory_space=pl.ANY)] * 7,
        out_specs=(pl.BlockSpec(memory_space=pltpu.VMEM),) * 2,
        scratch_shapes=[
            pltpu.VMEM((CTX, ROWS, FEAT), BF16),
            pltpu.VMEM((SEQ, 2 * HD), BF16),
            pltpu.VMEM((SEQ, HD), BF16),
            pltpu.VMEM((SEQ, 2 * HD), BF16),
            pltpu.VMEM((FEAT, COLS), BF16),
            pltpu.VMEM((FEAT, COLS), BF16),
            pltpu.VMEM((FEAT, COLS), BF16),
            pltpu.VMEM((FEAT, SEQ), BF16),
            pltpu.VMEM((4, ROWS, COLS), F32),
            pltpu.VMEM((4, ROWS, COLS), F32),
            pltpu.VMEM((4, ROWS, COLS), F32),
            pltpu.VMEM((CHIPS, HALF, HD), BF16),
            pltpu.VMEM((CHIPS, HALF, HD), BF16),
            pltpu.VMEM((2, HALF, HD), BF16),
            pltpu.VMEM((HD, SEQ), BF16),
            pltpu.VMEM((SEQ, HD), F32),
            pltpu.VMEM((HALF, HD), F32),
            pltpu.VMEM((CHIPS, SEQ, HD), BF16),
            pltpu.VMEM((CHIPS, FEAT, HD), F32),
            pltpu.VMEM((CHIPS, FEAT, HD), BF16),
            pltpu.VMEM((CHIPS, FEAT, HD), BF16),
            pltpu.VMEM((FEAT, COLS), BF16),
            dma(8), dma(8), dma(8), dma(8), dma(8), dma(8), dma(8), dma(8),
            dma(1), dma(1), dma(4), dma(4), dma(4), dma(4),
            dma(1), dma(1), dma(1), dma(1), dma(4), dma(4), dma(4), dma(4), dma(4), dma(4), dma(3),
        ],
        compiler_params=pltpu.CompilerParams(
            collective_id=0, has_side_effects=True, vmem_limit_bytes=56 * 1024 * 1024
        ),
    )(
        activations[0], queries[0], key_states[0], targets[0],
        value_weight[0], tracker[0], old_gradient[0],
    )
    return new_weight[None], new_tracker[None]


def solution(mesh):
    spec = P("rep", "ctx", None)
    return jax.shard_map(
        local, mesh=mesh, in_specs=(spec,) * 7, out_specs=(spec, spec), check_vma=False
    )
```

time: 347 us -> 150 us (0.43)
  the two profiles are of different devices: /device:TPU:1 before, /device:TPU:123 now
where the time goes in v1:
time: 150 us
  Pallas kernels  146 us (97%)
  local copies, waits for them, and re-layouts  2.72 us (2%)
    pallas_call x1, Pallas kernels, local(): pl.pallas_call(kernel, out_shape=(shape, shape), in_specs=[pl.BlockSpec(m...  146 us

profile of v1, /device:TPU:123, one launch (start us, length us, event | category | flops | bytes accessed | tf_op | source)
XLA Modules:
  0.0 149.6 jit_solution(483873678438204061)
XLA Ops:
  0.6 146.2 %shard_map.86 = (bf16[512,512]{1,0:T(8,128)(2,1)}, bf16[512,512]{1,0:T(8,128)(2,1)}) custom-call(bf16[128,4096]{1,0:T(8,128)(2,1)} %bitcast.9, bf16[128,2048]{1,0:T(8,128)(2,1)} %bitcast.12, bf16[128,512]{1,0:T(8,128)(2,1)} %bitcast.17, bf16[128,2048]{1,0:T(8,128)(2,1)} %bitcast.13, bf16[512,512]{1,0:T(8,128)(2,1)} %bitcast.14, bf16[512,512]{1,0:T(8,128)(2,1)} %bitcast.15, ...), custom_call_target="tpu_custom_call" | custom-call | tf_op jit(solution)/shard_map/pallas_call | solution.py:211
  146.9 0.0 copy-start
  146.9 1.9 %copy.11 = bf16[1,512,512]{2,1,0:T(8,128)(2,1)} copy(bf16[1,512,512]{2,1,0:T(8,128)(2,1)} %bitcast.11) | data formatting | bytes 1048576
  148.8 0.0 copy-done
  148.8 0.8 copy.12
Async XLA Ops:
  146.9 1.9 %copy-start = (bf16[512,512]{1,0:T(8,128)(2,1)S(1)}, bf16[512,512]{1,0:T(8,128)(2,1)}, u32[]{:S(2)}) copy-start(bf16[512,512]{1,0:T(8,128)(2,1)} %get-tuple-element.5) | copy-start | bytes 1572868

commit v2 on v1

v2 whole, which is shorter than its diff:
```python
import jax
import jax.numpy as jnp
from jax import lax
from jax.experimental import pallas as pl
from jax.experimental.pallas import tpu as pltpu
from jax.sharding import PartitionSpec as P

ROUND = 3
STEP = 0.25
LOSS = 16.0
CTX = 8
CHIPS = 4
ROWS = 128
SEQ = 1024
HALF = 512
D = 4096
FEAT = 512
COLS = 512
HD = 128
GROUP = 4
QB = 256
LOG2E = 1.4426950408889634
FILL = (2, 1, 1, 0)
F32 = jnp.float32
BF16 = jnp.bfloat16
MESH = pl.DeviceIdType.MESH


def dot(a, b):
    return jnp.dot(a, b, preferred_element_type=F32)


def dot_nt(a, b):
    return lax.dot_general(a, b, (((1,), (1,)), ((), ())), preferred_element_type=F32)


def kernel(
    a_h, q_h, k_h, t_h, w_h, tr_h, og_h,
    nw_ref, nt_ref,
    abuf, qbuf, kbuf, tbuf, wv, trv, ogv, ft, part, pin, sums, rbuf,
    v, vt, pt, cot, cross, trecv, vc, th, th16, thp, wp,
    a_s, a_r, q_s, q_r, k_s, k_r, t_s, t_r, w_s, w_r, p_s, p_r, r_s, r_r,
    v_s, v_r, c_s, c_r, g_s, g_r, m_s, m_r, x_s, x_r, loc,
):
    me = lax.axis_index("ctx")
    rep = lax.axis_index("rep")
    i = lax.div(me, 2)
    s = lax.rem(me, 2)
    p = lax.div(me, 4)
    a = lax.rem(i, 2)
    e = lax.rem(me, 4)
    q = 1 - p
    mate = me + 1 - 2 * s
    apart = 1 << ROUND
    peer = rep + apart * (1 - 2 * lax.rem(lax.div(rep, apart), 2))

    def dev(x, aa, ss):
        return 4 * x + 2 * aa + ss

    def lanes(n, size):
        return pl.ds(pl.multiple_of(n * size, size), size)

    def remote(src, dst, ss, rs, ctx, r=None):
        return pltpu.make_async_remote_copy(
            src_ref=src, dst_ref=dst, send_sem=ss, recv_sem=rs,
            device_id=(rep if r is None else r, ctx), device_id_type=MESH,
        )

    def arrived(ref, sem):
        pltpu.make_async_copy(ref, ref, sem).wait()

    barrier = pltpu.get_barrier_semaphore()
    pl.semaphore_signal(barrier, inc=1, device_id=(peer, me), device_id_type=MESH)
    for k in range(1, CTX):
        pl.semaphore_signal(barrier, inc=1, device_id=(rep, lax.rem(me + k, CTX)), device_id_type=MESH)

    mine = lanes(me, ROWS)
    here = lanes(e, ROWS)
    own = [
        pltpu.make_async_copy(w_h, wv, loc.at[0]),
        pltpu.make_async_copy(a_h.at[:, lanes(me, FEAT)], abuf.at[me], a_r.at[me]),
        pltpu.make_async_copy(k_h.at[:, lanes(e, HD)], kbuf.at[mine], k_r.at[me]),
        pltpu.make_async_copy(q_h.at[:, lanes(e, GROUP * HD)], qbuf.at[here], q_r.at[e]),
        pltpu.make_async_copy(t_h.at[:, lanes(e, GROUP * HD)], tbuf.at[here], t_r.at[e]),
        pltpu.make_async_copy(tr_h, trv, loc.at[1]),
        pltpu.make_async_copy(og_h, ogv, loc.at[2]),
    ]
    for copy in own:
        copy.start()

    pl.semaphore_wait(barrier, CTX)

    sends = []

    def send(*args):
        copy = remote(*args)
        copy.start()
        sends.append(copy)

    near = [dev(p, 1 - a, s), dev(p, 1 - a, 1 - s), mate]
    far = [dev(q, 1 - a, s), dev(q, 1 - a, 1 - s), dev(q, a, s), dev(q, a, 1 - s)]
    for n, to in enumerate(far + near):
        send(a_h.at[:, lanes(to, FEAT)], abuf.at[me], a_s.at[n], a_r.at[me], to)
    k_out = []
    for n, to in enumerate(far):
        k_out.append(remote(k_h.at[:, lanes(lax.rem(to, 4), HD)], kbuf.at[mine], k_s.at[n], k_r.at[me], to))

    @pl.when(p == 0)
    def _():
        for copy in k_out:
            copy.start()

    for n, to in enumerate(near):
        send(k_h.at[:, lanes(lax.rem(to, 4), HD)], kbuf.at[mine], k_s.at[4 + n], k_r.at[me], to)
    for n, to in enumerate(near):
        send(q_h.at[:, lanes(lax.rem(to, 4), GROUP * HD)], qbuf.at[here], q_s.at[n], q_r.at[e], to)
    for n, to in enumerate(near):
        send(t_h.at[:, lanes(lax.rem(to, 4), GROUP * HD)], tbuf.at[here], t_s.at[n], t_r.at[e], to)

    own[0].wait()
    for x, swap in ((p, 0), (q, 1)):
        rows = lanes(x, HALF)
        for m in range(4):
            j = 4 * x + m
            arrived(abuf.at[j], a_r.at[j])
            product = dot(abuf[j], wv[...])
            for h in range(4):
                part[h, lanes(j, ROWS), :] = product[:, h * HD:(h + 1) * HD]
            if m % 2:
                quarter = lanes(2 * x + m // 2, 2 * ROWS)
                for b in range(2):
                    n = 4 * swap + 2 * (m // 2) + b
                    send(part.at[2 * b + 1 - s, quarter], pin.at[b, quarter], p_s.at[n], p_r.at[n], mate)
        for m in range(4):
            j = 4 * x + m
            ft[:, lanes(j, ROWS)] = abuf[j].T
        for m in range(2):
            quarter = lanes(2 * x + m, 2 * ROWS)
            for b in range(2):
                n = 4 * swap + 2 * m + b
                arrived(pin.at[b, quarter], p_r.at[n])
                sums[x, b, m * 2 * ROWS:(m + 1) * 2 * ROWS, :] = (
                    part[2 * b + s, quarter, :] + pin[b, quarter, :]
                ).astype(BF16)
        if swap == 0:
            send(sums.at[p, 1 - a], rbuf.at[i], r_s.at[0], r_r.at[i], dev(p, 1 - a, s))
        else:
            send(sums.at[q, 1 - a], rbuf.at[i], r_s.at[1], r_r.at[i], dev(q, 1 - a, s))
            send(sums.at[q, a], rbuf.at[i], r_s.at[2], r_r.at[i], dev(q, a, s))

    chunk = [0]

    def fill(n):
        for _ in range(n):
            rows = pl.ds(chunk[0] * ROWS, ROWS)
            send(w_h.at[rows], wp.at[rows], w_s.at[chunk[0]], w_r.at[chunk[0]], me, peer)
            chunk[0] += 1

    fill(FILL[0])

    for n in range(4):
        rows = pl.ds(n * ROWS, ROWS)
        arrived(qbuf.at[rows], q_r.at[n])
    later = lax.broadcasted_iota(jnp.int32, (QB, QB), 0) > lax.broadcasted_iota(jnp.int32, (QB, QB), 1)

    def softmax(base):
        def head(g, carry):
            for b in range(HALF // QB):
                upto = base + (b + 1) * QB
                scores = dot_nt(kbuf[:upto, :], qbuf[b * QB:(b + 1) * QB, lanes(g, HD)])
                edge = jnp.where(later, -jnp.inf, scores[upto - QB:, :])
                scores = jnp.concatenate((scores[:upto - QB, :], edge), axis=0) if upto > QB else edge
                highest = jnp.max(scores, axis=0, keepdims=True)
                raised = jnp.exp2((scores - highest) * (HD ** -0.5 * LOG2E))
                share = 1.0 / jnp.sum(raised, axis=0, keepdims=True)
                cols = lanes(2 * g + b, QB)
                pt[:upto, cols] = (raised * share).astype(BF16)
                if upto < base + HALF:
                    pt[upto:base + HALF, cols] = jnp.zeros((base + HALF - upto, QB), BF16)
            return carry

        lax.fori_loop(0, GROUP, head, 0)

    for j in range(4):
        arrived(kbuf.at[pl.ds(j * ROWS, ROWS)], k_r.at[j])

    @pl.when(p == 0)
    def _():
        softmax(0)

    @pl.when(p == 1)
    def _():
        for j in range(4, CTX):
            arrived(kbuf.at[pl.ds(j * ROWS, ROWS)], k_r.at[j])
        softmax(HALF)

    for other in (2 * p + 1 - a, 2 * q + a, 2 * q + 1 - a):
        arrived(rbuf.at[other], r_r.at[other])
    for m in range(2):
        rows = slice(m * 2 * ROWS, (m + 1) * 2 * ROWS)
        quarter = lanes(2 * p + m, 2 * ROWS)
        total = part[e, quarter, :] + pin[a, quarter, :]
        for other in (2 * p + 1 - a, 2 * q + a, 2 * q + 1 - a):
            total = total + rbuf[other, rows, :].astype(F32)
        v[p, rows, :] = (total * D ** -0.5).astype(BF16)
    onward = remote(v.at[0], v.at[0], v_s.at[0], v_r.at[0], dev(1, a, s))

    @pl.when(p == 0)
    def _():
        onward.start()

    fill(FILL[1])
    vt[:, lanes(p, HALF)] = v[p].T
    for n in range(4):
        rows = pl.ds(n * ROWS, ROWS)
        arrived(tbuf.at[rows], t_r.at[n])

    def attend(base):
        def head(g, carry):
            for b in range(HALF // QB):
                upto = base + (b + 1) * QB
                n = lanes(2 * g + b, QB)
                attended = dot(vt[:, :upto], pt[:upto, n]).T
                wanted = tbuf[b * QB:(b + 1) * QB, lanes(g, HD)].astype(F32)
                cot[n, :] = (LOSS * (attended - wanted)).astype(BF16)
            return carry

        lax.fori_loop(0, GROUP, head, 0)

    @pl.when(p == 0)
    def _():
        attend(0)
        terms = dot(pt[:HALF, :], cot[...])
        arrived(trecv, c_r.at[0])
        vc[e, :HALF, :] = (terms + trecv[...].astype(F32)).astype(BF16)

    back = remote(cross, trecv, c_s.at[0], c_r.at[0], dev(0, a, s))

    @pl.when(p == 1)
    def _():
        arrived(v.at[0], v_r.at[0])
        vt[:, :HALF] = v[0].T
        attend(HALF)
        cross[...] = dot(pt[:HALF, :], cot[...]).astype(BF16)
        back.start()
        vc[e, HALF:, :] = dot(pt[HALF:, :], cot[...]).astype(BF16)

    def block(x, aa, ss):
        return vc.at[2 * aa + ss, lanes(x, HALF)]

    send(block(p, a, s), block(p, a, s), g_s.at[0], g_r.at[i], dev(q, a, s))
    send(block(p, a, s), block(p, a, s), g_s.at[1], g_r.at[i], dev(p, 1 - a, s))
    send(block(p, a, s), block(p, a, s), m_s.at[0], m_r.at[i], mate)
    fill(FILL[2])

    own[5].wait()
    own[6].wait()

    def gradient(n, h):
        cols = lanes(h, HD)
        grad = dot(ft[...], vc[h]) * D ** -0.5
        stepped = trv[:, cols].astype(F32) + grad - ogv[:, cols].astype(F32)
        th[h] = stepped
        th16[h] = stepped.astype(BF16)
        send(th16.at[h], thp.at[h], x_s.at[n], x_r.at[h], me, peer)

    def landed(x, aa):
        arrived(block(x, aa, s), g_r.at[2 * x + aa])

    def passed(x, aa):
        arrived(block(x, aa, 1 - s), m_r.at[2 * x + aa])

    def forward(n, x, aa):
        send(block(x, aa, s), block(x, aa, s), m_s.at[n], m_r.at[2 * x + aa], mate)

    landed(q, a)
    send(block(q, a, s), block(q, a, s), g_s.at[2], g_r.at[2 * q + a], dev(p, 1 - a, s))
    forward(1, q, a)
    gradient(0, e)
    landed(p, 1 - a)
    forward(2, p, 1 - a)
    passed(p, a)
    passed(q, a)
    gradient(1, 2 * a + 1 - s)
    landed(q, 1 - a)
    forward(3, q, 1 - a)
    gradient(2, 2 * (1 - a) + s)
    passed(p, 1 - a)
    passed(q, 1 - a)
    gradient(3, 2 * (1 - a) + 1 - s)
    fill(FILL[3])

    for n in range(4):
        rows = pl.ds(n * ROWS, ROWS)
        arrived(wp.at[rows], w_r.at[n])
    for h in (e, 2 * a + 1 - s, 2 * (1 - a) + s, 2 * (1 - a) + 1 - s):
        cols = lanes(h, HD)
        arrived(thp.at[h], x_r.at[h])
        mixed = (th[h] + thp[h].astype(F32)) * 0.5
        nt_ref[:, cols] = mixed.astype(BF16)
        nw_ref[:, cols] = (
            (wv[:, cols].astype(F32) + wp[:, cols].astype(F32)) * 0.5 - STEP * mixed
        ).astype(BF16)
    for copy in sends:
        copy.wait_send()

    @pl.when(p == 0)
    def _():
        onward.wait_send()
        for copy in k_out:
            copy.wait_send()

    @pl.when(p == 1)
    def _():
        back.wait_send()


def local(activations, queries, key_states, targets, value_weight, tracker, old_gradient):
    dma = lambda n: pltpu.SemaphoreType.DMA((n,))
    shape = jax.ShapeDtypeStruct((FEAT, COLS), BF16)
    new_weight, new_tracker = pl.pallas_call(
        kernel,
        out_shape=(shape, shape),
        in_specs=[pl.BlockSpec(memory_space=pl.ANY)] * 7,
        out_specs=(pl.BlockSpec(memory_space=pltpu.VMEM),) * 2,
        scratch_shapes=[
            pltpu.VMEM((CTX, ROWS, FEAT), BF16),
            pltpu.VMEM((HALF, GROUP * HD), BF16),
            pltpu.VMEM((SEQ, HD), BF16),
            pltpu.VMEM((HALF, GROUP * HD), BF16),
            pltpu.VMEM((FEAT, COLS), BF16),
            pltpu.VMEM((FEAT, COLS), BF16),
            pltpu.VMEM((FEAT, COLS), BF16),
            pltpu.VMEM((FEAT, SEQ), BF16),
            pltpu.VMEM((4, SEQ, HD), F32),
            pltpu.VMEM((2, SEQ, HD), F32),
            pltpu.VMEM((2, 2, HALF, HD), BF16),
            pltpu.VMEM((CHIPS, HALF, HD), BF16),
            pltpu.VMEM((2, HALF, HD), BF16),
            pltpu.VMEM((HD, SEQ), BF16),
            pltpu.VMEM((SEQ, GROUP * HALF), BF16),
            pltpu.VMEM((GROUP * HALF, HD), BF16),
            pltpu.VMEM((HALF, HD), BF16),
            pltpu.VMEM((HALF, HD), BF16),
            pltpu.VMEM((4, SEQ, HD), BF16),
            pltpu.VMEM((4, FEAT, HD), F32),
            pltpu.VMEM((4, FEAT, HD), BF16),
            pltpu.VMEM((4, FEAT, HD), BF16),
            pltpu.VMEM((FEAT, COLS), BF16),
            dma(7), dma(8), dma(3), dma(4), dma(7), dma(8), dma(3), dma(4),
            dma(4), dma(4), dma(8), dma(8), dma(3), dma(4),
            dma(1), dma(1), dma(1), dma(1), dma(3), dma(4), dma(4), dma(4), dma(4), dma(4), dma(3),
        ],
        compiler_params=pltpu.CompilerParams(
            collective_id=0, has_side_effects=True, vmem_limit_bytes=56 * 1024 * 1024
        ),
    )(
        activations[0], queries[0], key_states[0], targets[0],
        value_weight[0], tracker[0], old_gradient[0],
    )
    return new_weight[None], new_tracker[None]


def solution(mesh):
    spec = P("rep", "ctx", None)
    return jax.shard_map(
        local, mesh=mesh, in_specs=(spec,) * 7, out_specs=(spec, spec), check_vma=False
    )
```

time: 150 us -> 124 us (0.83)
  the two profiles are of different devices: /device:TPU:123 before, /device:TPU:250 now
where the time goes in v2:
time: 124 us
  Pallas kernels  121 us (98%)
  local copies, waits for them, and re-layouts  2.72 us (2%)
    pallas_call x1, Pallas kernels, local(): pl.pallas_call(kernel, out_shape=(shape, shape), in_specs=[pl.BlockSpec(m...  121 us
    unnamed x4, local copies, waits for them, and re-layouts  2.72 us

profile of v2, /device:TPU:250, one launch (start us, length us, event | category | flops | bytes accessed | tf_op | source)
XLA Modules:
  0.0 124.0 jit_solution(10739804985497523063)
XLA Ops:
  0.6 120.6 %shard_map.86 = (bf16[512,512]{1,0:T(8,128)(2,1)}, bf16[512,512]{1,0:T(8,128)(2,1)}) custom-call(bf16[128,4096]{1,0:T(8,128)(2,1)} %bitcast.9, bf16[128,2048]{1,0:T(8,128)(2,1)} %bitcast.12, bf16[128,512]{1,0:T(8,128)(2,1)} %bitcast.17, bf16[128,2048]{1,0:T(8,128)(2,1)} %bitcast.13, bf16[512,512]{1,0:T(8,128)(2,1)} %bitcast.14, bf16[512,512]{1,0:T(8,128)(2,1)} %bitcast.15, ...), custom_call_target="tpu_custom_call" | custom-call | tf_op jit(solution)/shard_map/pallas_call | solution.py:321
  121.3 0.0 copy-start
  121.3 1.9 %copy.11 = bf16[1,512,512]{2,1,0:T(8,128)(2,1)} copy(bf16[1,512,512]{2,1,0:T(8,128)(2,1)} %bitcast.11) | data formatting | bytes 1048576
  123.2 0.0 copy-done
  123.2 0.8 copy.12
Async XLA Ops:
  121.3 1.9 %copy-start = (bf16[512,512]{1,0:T(8,128)(2,1)S(1)}, bf16[512,512]{1,0:T(8,128)(2,1)}, u32[]{:S(2)}) copy-start(bf16[512,512]{1,0:T(8,128)(2,1)} %get-tuple-element.5) | copy-start | bytes 1572868

commit v3 on v2

--- a/solution.py
+++ b/solution.py
@@ -20,7 +20,7 @@
 GROUP = 4
 QB = 256
 LOG2E = 1.4426950408889634
-FILL = (2, 1, 1, 0)
+FILL = (1, 2, 1, 0)
 F32 = jnp.float32
 BF16 = jnp.bfloat16
 MESH = pl.DeviceIdType.MESH
@@ -36,9 +36,9 @@
 
 def kernel(
     a_h, q_h, k_h, t_h, w_h, tr_h, og_h,
-    nw_ref, nt_ref,
+    th_out, thp_out, wp_out,
     abuf, qbuf, kbuf, tbuf, wv, trv, ogv, ft, part, pin, sums, rbuf,
-    v, vt, pt, cot, cross, trecv, vc, th, th16, thp, wp,
+    v, vt, pt, cot, cross, trecv, vc, th, th16,
     a_s, a_r, q_s, q_r, k_s, k_r, t_s, t_r, w_s, w_r, p_s, p_r, r_s, r_r,
     v_s, v_r, c_s, c_r, g_s, g_r, m_s, m_r, x_s, x_r, loc,
 ):
@@ -114,9 +114,6 @@
         send(k_h.at[:, lanes(lax.rem(to, 4), HD)], kbuf.at[mine], k_s.at[4 + n], k_r.at[me], to)
     for n, to in enumerate(near):
         send(q_h.at[:, lanes(lax.rem(to, 4), GROUP * HD)], qbuf.at[here], q_s.at[n], q_r.at[e], to)
-    for n, to in enumerate(near):
-        send(t_h.at[:, lanes(lax.rem(to, 4), GROUP * HD)], tbuf.at[here], t_s.at[n], t_r.at[e], to)
-
     own[0].wait()
     for x, swap in ((p, 0), (q, 1)):
         rows = lanes(x, HALF)
@@ -153,9 +150,11 @@
     def fill(n):
         for _ in range(n):
             rows = pl.ds(chunk[0] * ROWS, ROWS)
-            send(w_h.at[rows], wp.at[rows], w_s.at[chunk[0]], w_r.at[chunk[0]], me, peer)
+            send(w_h.at[rows], wp_out.at[rows], w_s.at[chunk[0]], w_r.at[chunk[0]], me, peer)
             chunk[0] += 1
 
+    for n, to in enumerate(near):
+        send(t_h.at[:, lanes(lax.rem(to, 4), GROUP * HD)], tbuf.at[here], t_s.at[n], t_r.at[e], to)
     fill(FILL[0])
 
     for n in range(4):
@@ -256,13 +255,18 @@
     own[5].wait()
     own[6].wait()
 
+    kept = []
+
     def gradient(n, h):
         cols = lanes(h, HD)
         grad = dot(ft[...], vc[h]) * D ** -0.5
         stepped = trv[:, cols].astype(F32) + grad - ogv[:, cols].astype(F32)
         th[h] = stepped
         th16[h] = stepped.astype(BF16)
-        send(th16.at[h], thp.at[h], x_s.at[n], x_r.at[h], me, peer)
+        send(th16.at[h], thp_out.at[:, cols], x_s.at[n], x_r.at[n], me, peer)
+        keep = pltpu.make_async_copy(th.at[h], th_out.at[:, cols], loc.at[3 + n])
+        keep.start()
+        kept.append(keep)
 
     def landed(x, aa):
         arrived(block(x, aa, s), g_r.at[2 * x + aa])
@@ -292,15 +296,10 @@
 
     for n in range(4):
         rows = pl.ds(n * ROWS, ROWS)
-        arrived(wp.at[rows], w_r.at[n])
-    for h in (e, 2 * a + 1 - s, 2 * (1 - a) + s, 2 * (1 - a) + 1 - s):
-        cols = lanes(h, HD)
-        arrived(thp.at[h], x_r.at[h])
-        mixed = (th[h] + thp[h].astype(F32)) * 0.5
-        nt_ref[:, cols] = mixed.astype(BF16)
-        nw_ref[:, cols] = (
-            (wv[:, cols].astype(F32) + wp[:, cols].astype(F32)) * 0.5 - STEP * mixed
-        ).astype(BF16)
+        arrived(wp_out.at[rows], w_r.at[n])
+    for n, h in enumerate((e, 2 * a + 1 - s, 2 * (1 - a) + s, 2 * (1 - a) + 1 - s)):
+        kept[n].wait()
+        arrived(thp_out.at[:, lanes(h, HD)], x_r.at[n])
     for copy in sends:
         copy.wait_send()
 
@@ -317,12 +316,12 @@
 
 def local(activations, queries, key_states, targets, value_weight, tracker, old_gradient):
     dma = lambda n: pltpu.SemaphoreType.DMA((n,))
-    shape = jax.ShapeDtypeStruct((FEAT, COLS), BF16)
-    new_weight, new_tracker = pl.pallas_call(
+    half = jax.ShapeDtypeStruct((FEAT, COLS), BF16)
+    th, peer_th, peer_weight = pl.pallas_call(
         kernel,
-        out_shape=(shape, shape),
+        out_shape=(jax.ShapeDtypeStruct((FEAT, COLS), F32), half, half),
         in_specs=[pl.BlockSpec(memory_space=pl.ANY)] * 7,
-        out_specs=(pl.BlockSpec(memory_space=pltpu.VMEM),) * 2,
+        out_specs=(pl.BlockSpec(memory_space=pl.ANY),) * 3,
         scratch_shapes=[
             pltpu.VMEM((CTX, ROWS, FEAT), BF16),
             pltpu.VMEM((HALF, GROUP * HD), BF16),
@@ -345,11 +344,9 @@
             pltpu.VMEM((4, SEQ, HD), BF16),
             pltpu.VMEM((4, FEAT, HD), F32),
             pltpu.VMEM((4, FEAT, HD), BF16),
-            pltpu.VMEM((4, FEAT, HD), BF16),
-            pltpu.VMEM((FEAT, COLS), BF16),
             dma(7), dma(8), dma(3), dma(4), dma(7), dma(8), dma(3), dma(4),
             dma(4), dma(4), dma(8), dma(8), dma(3), dma(4),
-            dma(1), dma(1), dma(1), dma(1), dma(3), dma(4), dma(4), dma(4), dma(4), dma(4), dma(3),
+            dma(1), dma(1), dma(1), dma(1), dma(3), dma(4), dma(4), dma(4), dma(4), dma(4), dma(7),
         ],
         compiler_params=pltpu.CompilerParams(
             collective_id=0, has_side_effects=True, vmem_limit_bytes=56 * 1024 * 1024
@@ -358,7 +355,9 @@
         activations[0], queries[0], key_states[0], targets[0],
         value_weight[0], tracker[0], old_gradient[0],
     )
-    return new_weight[None], new_tracker[None]
+    mixed = (th + peer_th.astype(F32)) * 0.5
+    weights = (value_weight[0].astype(F32) + peer_weight.astype(F32)) * 0.5
+    return (weights - STEP * mixed).astype(BF16)[None], mixed.astype(BF16)[None]
 
 
 def solution(mesh):

time: 124 us -> 118 us (0.952)
  the two profiles are of different devices: /device:TPU:250 before, /device:TPU:190 now
where the time goes in v3:
time: 118 us
  Pallas kernels  115 us (97%)
  other arithmetic  2.84 us (2%)
    pallas_call x1, Pallas kernels, local(): pl.pallas_call(kernel, out_shape=(jax.ShapeDtypeStruct((FEAT, COLS), F32)...  115 us
    broadcast_in_dim x1, other arithmetic, local(): mixed.astype(BF16)[None]  2.84 us

profile of v3, /device:TPU:190, one launch (start us, length us, event | category | flops | bytes accessed | tf_op | source)
XLA Modules:
  0.0 118.3 jit_solution(5010359351319350605)
XLA Ops:
  0.6 0.0 copy-start
  0.6 114.8 %shard_map.86 = (f32[512,512]{1,0:T(8,128)}, bf16[512,512]{1,0:T(8,128)(2,1)}, bf16[512,512]{1,0:T(8,128)(2,1)}) custom-call(bf16[128,4096]{1,0:T(8,128)(2,1)} %bitcast.13, bf16[128,2048]{1,0:T(8,128)(2,1)} %bitcast.14, bf16[128,512]{1,0:T(8,128)(2,1)} %bitcast.18, bf16[128,2048]{1,0:T(8,128)(2,1)} %bitcast.15, bf16[512,512]{1,0:T(8,128)(2,1)} %bitcast.12, ...), custom_call_target="tpu_custom_call" | custom-call | tf_op jit(solution)/shard_map/pallas_call | solution.py:320
  115.4 0.0 copy-done
  115.4 2.8 %fusion.1 = (bf16[1,512,512]{2,1,0:T(8,128)(2,1)}, bf16[1,512,512]{2,1,0:T(8,128)(2,1)}) fusion(f32[512,512]{1,0:T(8,128)} %get-tuple-element.6, bf16[512,512]{1,0:T(8,128)(2,1)} %get-tuple-element.7, bf16[512,512]{1,0:T(8,128)(2,1)} %get-tuple-element.5, bf16[1,512,512]{2,1,0:T(8,128)(2,1)S(1)} %copy-done), kind=kLoop, calls=%fused_computation.4 | loop fusion | flops 2883584 | bytes 3670016 | tf_op jit(solution)/shard_map/broadcast_in_dim | solution.py:360
Async XLA Ops:
  0.6 114.8 %copy-start = (bf16[1,512,512]{2,1,0:T(8,128)(2,1)S(1)}, bf16[1,512,512]{2,1,0:T(8,128)(2,1)}, u32[]{:S(2)}) copy-start(bf16[1,512,512]{2,1,0:T(8,128)(2,1)} %param.11) | copy-start | bytes 1572868

commit v4 on v3

--- a/solution.py
+++ b/solution.py
@@ -37,7 +37,7 @@
 def kernel(
     a_h, q_h, k_h, t_h, w_h, tr_h, og_h,
     th_out, thp_out, wp_out,
-    abuf, qbuf, kbuf, tbuf, wv, trv, ogv, ft, part, pin, sums, rbuf,
+    abuf, qbuf, kbuf, tbuf, wv, trv, ogv, ft, part, pout, pin, sums, rbuf,
     v, vt, pt, cot, cross, trecv, vc, th, th16,
     a_s, a_r, q_s, q_r, k_s, k_r, t_s, t_r, w_s, w_r, p_s, p_r, r_s, r_r,
     v_s, v_r, c_s, c_r, g_s, g_r, m_s, m_r, x_s, x_r, loc,
@@ -127,7 +127,8 @@
                 quarter = lanes(2 * x + m // 2, 2 * ROWS)
                 for b in range(2):
                     n = 4 * swap + 2 * (m // 2) + b
-                    send(part.at[2 * b + 1 - s, quarter], pin.at[b, quarter], p_s.at[n], p_r.at[n], mate)
+                    pout[b, quarter, :] = part[2 * b + 1 - s, quarter, :].astype(BF16)
+                    send(pout.at[b, quarter], pin.at[b, quarter], p_s.at[n], p_r.at[n], mate)
         for m in range(4):
             j = 4 * x + m
             ft[:, lanes(j, ROWS)] = abuf[j].T
@@ -137,7 +138,7 @@
                 n = 4 * swap + 2 * m + b
                 arrived(pin.at[b, quarter], p_r.at[n])
                 sums[x, b, m * 2 * ROWS:(m + 1) * 2 * ROWS, :] = (
-                    part[2 * b + s, quarter, :] + pin[b, quarter, :]
+                    part[2 * b + s, quarter, :] + pin[b, quarter, :].astype(F32)
                 ).astype(BF16)
         if swap == 0:
             send(sums.at[p, 1 - a], rbuf.at[i], r_s.at[0], r_r.at[i], dev(p, 1 - a, s))
@@ -198,7 +199,7 @@
     for m in range(2):
         rows = slice(m * 2 * ROWS, (m + 1) * 2 * ROWS)
         quarter = lanes(2 * p + m, 2 * ROWS)
-        total = part[e, quarter, :] + pin[a, quarter, :]
+        total = part[e, quarter, :] + pin[a, quarter, :].astype(F32)
         for other in (2 * p + 1 - a, 2 * q + a, 2 * q + 1 - a):
             total = total + rbuf[other, rows, :].astype(F32)
         v[p, rows, :] = (total * D ** -0.5).astype(BF16)
@@ -332,7 +333,8 @@
             pltpu.VMEM((FEAT, COLS), BF16),
             pltpu.VMEM((FEAT, SEQ), BF16),
             pltpu.VMEM((4, SEQ, HD), F32),
-            pltpu.VMEM((2, SEQ, HD), F32),
+            pltpu.VMEM((2, SEQ, HD), BF16),
+            pltpu.VMEM((2, SEQ, HD), BF16),
             pltpu.VMEM((2, 2, HALF, HD), BF16),
             pltpu.VMEM((CHIPS, HALF, HD), BF16),
             pltpu.VMEM((2, HALF, HD), BF16),

time: 118 us -> 118 us (level)
  no operation moved by 1% of the time
where the time goes in v4:
time: 118 us
  Pallas kernels  115 us (97%)
  other arithmetic  2.84 us (2%)
    pallas_call x1, Pallas kernels, local(): pl.pallas_call(kernel, out_shape=(jax.ShapeDtypeStruct((FEAT, COLS), F32)...  115 us
    broadcast_in_dim x1, other arithmetic, local(): mixed.astype(BF16)[None]  2.84 us

profile of v4, /device:TPU:190, one launch (start us, length us, event | category | flops | bytes accessed | tf_op | source)
XLA Modules:
  0.0 118.3 jit_solution(456919099056844558)
XLA Ops:
  0.6 0.0 copy-start
  0.6 114.9 %shard_map.86 = (f32[512,512]{1,0:T(8,128)}, bf16[512,512]{1,0:T(8,128)(2,1)}, bf16[512,512]{1,0:T(8,128)(2,1)}) custom-call(bf16[128,4096]{1,0:T(8,128)(2,1)} %bitcast.13, bf16[128,2048]{1,0:T(8,128)(2,1)} %bitcast.14, bf16[128,512]{1,0:T(8,128)(2,1)} %bitcast.18, bf16[128,2048]{1,0:T(8,128)(2,1)} %bitcast.15, bf16[512,512]{1,0:T(8,128)(2,1)} %bitcast.12, ...), custom_call_target="tpu_custom_call" | custom-call | tf_op jit(solution)/shard_map/pallas_call | solution.py:321
  115.5 0.0 copy-done
  115.5 2.8 %fusion.1 = (bf16[1,512,512]{2,1,0:T(8,128)(2,1)}, bf16[1,512,512]{2,1,0:T(8,128)(2,1)}) fusion(f32[512,512]{1,0:T(8,128)} %get-tuple-element.6, bf16[512,512]{1,0:T(8,128)(2,1)} %get-tuple-element.7, bf16[512,512]{1,0:T(8,128)(2,1)} %get-tuple-element.5, bf16[1,512,512]{2,1,0:T(8,128)(2,1)S(1)} %copy-done), kind=kLoop, calls=%fused_computation.4 | loop fusion | flops 2883584 | bytes 3670016 | tf_op jit(solution)/shard_map/broadcast_in_dim | solution.py:362
Async XLA Ops:
  0.6 114.9 %copy-start = (bf16[1,512,512]{2,1,0:T(8,128)(2,1)S(1)}, bf16[1,512,512]{2,1,0:T(8,128)(2,1)}, u32[]{:S(2)}) copy-start(bf16[1,512,512]{2,1,0:T(8,128)(2,1)} %param.11) | copy-start | bytes 1572868
